TPU v7x, 32 devices: a whole 2x2x4 slice. The times are simulated.
32 devices in a mesh: gx: 8 (over z, y), gy: 4 (over x, core).
Axes of the slice: x: 2, y: 2, z: 4, core: 2. Of those that a mesh axis runs over, the one named last changes fastest.
Arguments:
- covariance: bfloat16 [4, 32, 32, 4096], P(None, 'gx', 'gy'), may hold values from -8 to 8, as said below
- pilot_ids: int32 [4, 32, 32], P(None, 'gx', 'gy'), may hold values from 0 to 15
- targets: float32 [2, 4, 32, 32], P(None, None, 'gx', 'gy'), may hold values from -6 to 6
- encoder_beam_weight: bfloat16 [64, 512], replicated, may hold values from -1 to 1
- norm_gain: float32 [512], replicated, may hold values from 0.5 to 1.5
- pilot_table: float32 [16, 512], replicated, may hold values from -3 to 3
- pair_weight: bfloat16 [512, 1024], replicated, may hold values from -0.25 to 0.25
- edge_bias: float32 [512], replicated, may hold values from -3 to 3
- node_weight: bfloat16 [1024, 512], replicated, may hold values from -0.1875 to 0.1875
- node_bias: float32 [512], replicated, may hold values from -3 to 3
- update_weight: bfloat16 [512, 512], replicated, may hold values from -0.25 to 0.25
- readout_weight: bfloat16 [2, 512], replicated, may hold values from -0.25 to 0.25
Outputs:
- estimates: float32 [2, 4, 32, 32], P(None, None, 'gx', 'gy')
- grad_pair_weight: float32 [512, 1024], P('gx')
- grad_node_weight: float32 [1024, 512], P('gx')
- grad_update_weight: float32 [512, 512], replicated
- grad_beam_weights: float32 [64, 512], replicated
- grad_edge_bias: float32 [512], replicated
- grad_node_bias: float32 [512], replicated
- grad_norm_gain: float32 [512], replicated
- grad_pilot_table: float32 [16, 512], replicated
- grad_readout_weight: float32 [2, 512], replicated
- point_gradient: float32 [4, 32, 32, 512], P(None, 'gx', 'gy')
Inputs may be any that keep to these rules, and one draw needn't show every extreme that they name: `covariance`: each access point's matrix, read as 64 x 64 row by row, is symmetric.
All inputs are finite; a program needn't handle non-finite values.
Results may differ from a plain program's by a relative error of at most 0.0095.
Values may be sent and summed in bfloat16 or wider, within the bound.
A program may use at most 64 MiB of HBM per device.

v0:
```python
import math

import jax
import jax.numpy as jnp
from jax import lax
from jax.sharding import PartitionSpec as P

ROUNDS = 3


EPSILON = 1e-06
GRID_STEPS = [(-1, -1), (-1, 0), (-1, 1), (0, -1), (0, 1), (1, -1), (1, 0), (1, 1)]
HIGHEST = lax.Precision.HIGHEST


def with_halo(cells, sides, width):
    for axis, dim in sides:
        count = lax.axis_size(axis)
        ends = count - 1
        head = lax.slice_in_dim(cells, 0, width, axis=dim)
        tail = lax.slice_in_dim(cells, cells.shape[dim] - width, cells.shape[dim], axis=dim)
        cells = jnp.concatenate(
            [
                lax.ppermute(tail, axis, [(i, (i + 1) % count) for i in range(ends)]),
                cells,
                lax.ppermute(head, axis, [((i + 1) % count, i) for i in range(ends)]),
            ],
            axis=dim,
        )
    return cells


def from_behind(value, axis, steps):
    count = lax.axis_size(axis)
    leading, last = (max(0, -steps), min(count, count - steps))
    return lax.ppermute(value, axis, [(source, source + steps) for source in range(leading, last)])


def silu_slope(values):
    sigmoid = jax.nn.sigmoid(values)
    return sigmoid * (1.0 + values * (1.0 - sigmoid))


def contract_rows(left_rows, right_rows):
    return lax.dot_general(
        left_rows, right_rows, (((0,), (0,)), ((), ())), preferred_element_type=jnp.float32
    )


def times_transpose(left_rows, right_cols):
    return lax.dot_general(
        left_rows, right_cols, (((1,), (1,)), ((), ())), preferred_element_type=jnp.float32
    )


def arrange(padded, distant, height, width):
    nearby = [
        padded[:, 1 + row_step : 1 + row_step + height, 1 + col_step : 1 + col_step + width]
        for row_step, col_step in GRID_STEPS
    ]
    return nearby + list(distant)


def validity(height, width, span_rows):
    row_first = lax.axis_index("gx") * height
    col_first = lax.axis_index("gy") * width
    total_rows = height * lax.axis_size("gx")
    total_cols = width * lax.axis_size("gy")
    rows_here = row_first + lax.broadcasted_iota(jnp.int32, (height, width), 0)
    cols_here = col_first + lax.broadcasted_iota(jnp.int32, (height, width), 1)
    masks = []
    for row_step, col_step in GRID_STEPS + [(span_rows, 0), (-span_rows, 0)]:
        inside = (
            (rows_here + row_step >= 0)
            & (rows_here + row_step < total_rows)
            & (cols_here + col_step >= 0)
            & (cols_here + col_step < total_cols)
        )
        masks.append(inside.astype(jnp.float32)[None, :, :, None])
    return masks


def fetch_forward(field, span):
    padded = with_halo(field, (("gx", 1), ("gy", 2)), 1)
    distant = [from_behind(field, "gx", moved_by) for moved_by in (-span, span)]
    return (padded, distant)


def fetch_pair(field, span):
    padded = with_halo(field, (("gx", 1), ("gy", 2)), 1)
    distant = [from_behind(field, "gx", moved_by) for moved_by in (-span, span)]
    return (padded, distant)


def on_device(
    covariance,
    pilot_ids,
    targets,
    encoder_beam_weight,
    norm_gain,
    pilot_table,
    pair_weight,
    edge_bias,
    node_weight,
    node_bias,
    update_weight,
    readout_weight,
):
    samples, height, width = (covariance.shape[0], covariance.shape[1], covariance.shape[2])
    antennas = encoder_beam_weight.shape[0]
    features = encoder_beam_weight.shape[1]
    pilots = pilot_table.shape[0]
    span = lax.axis_size("gx") // 4
    span_rows = span * height
    points = samples * height * width
    total_points = points * lax.axis_size("gx") * lax.axis_size("gy")
    masks = validity(height, width, span_rows)
    degree = masks[0]
    for another in masks[1:]:
        degree = degree + another
    beams = encoder_beam_weight.astype(jnp.float32)
    block_list = covariance.reshape(samples * height, width * antennas, antennas)

    def block_power(covariance_block):
        projected_beams = jnp.dot(
            covariance_block, encoder_beam_weight, preferred_element_type=jnp.float32
        ).reshape(width, antennas, features)
        return jnp.sum(projected_beams * beams[None], axis=1)

    powers = lax.map(block_power, block_list).reshape(samples, height, width, features)
    inverse = lax.rsqrt(jnp.mean(powers * powers, axis=-1, keepdims=True) + EPSILON)
    normed = powers * inverse
    onehot = (pilot_ids.reshape(points, 1) == jnp.arange(pilots, dtype=jnp.int32)[None, :]).astype(
        jnp.float32
    )
    looked = lax.dot_general(
        onehot,
        pilot_table,
        (((1,), (0,)), ((), ())),
        precision=HIGHEST,
        preferred_element_type=jnp.float32,
    )
    hidden = normed * norm_gain + looked.reshape(samples, height, width, features)
    saved = []
    for round_index in range(ROUNDS):
        flat_hidden = hidden.astype(jnp.bfloat16).reshape(points, features)
        pair_proj = jnp.dot(flat_hidden, pair_weight, preferred_element_type=jnp.float32).reshape(
            samples, height, width, 2 * features
        )
        query_part = pair_proj[..., :features].astype(jnp.bfloat16)
        key_part = pair_proj[..., features:].astype(jnp.bfloat16)
        padded, distant = fetch_forward(key_part, span)
        key_near = arrange(padded, distant, height, width)
        query_kept = None
        query_wide = query_part.astype(jnp.float32)
        edge_total = jnp.zeros((samples, height, width, features), jnp.float32)
        for inside, neighbour in zip(masks, key_near):
            edge_total = edge_total + inside * jax.nn.silu(
                query_wide + neighbour.astype(jnp.float32) + edge_bias
            )
        flat_message = (edge_total / degree).astype(jnp.bfloat16).reshape(points, features)
        before = (
            jnp.dot(flat_hidden, node_weight[:features], preferred_element_type=jnp.float32)
            + jnp.dot(flat_message, node_weight[features:], preferred_element_type=jnp.float32)
            + node_bias
        )
        update = jax.nn.silu(before).astype(jnp.bfloat16)
        hidden = hidden + jnp.dot(
            update, update_weight, preferred_element_type=jnp.float32
        ).reshape(samples, height, width, features)
        saved.append(
            (flat_hidden, query_part, key_part, key_near, query_kept, flat_message, before, update)
        )
    final_flat = hidden.astype(jnp.bfloat16).reshape(points, features)
    estimates = times_transpose(readout_weight, final_flat)
    residual_slope = (estimates - targets.reshape(2, points)) * (2.0 / math.sqrt(total_points))
    grad_readout = lax.dot_general(
        residual_slope,
        final_flat.astype(jnp.float32),
        (((1,), (0,)), ((), ())),
        precision=HIGHEST,
        preferred_element_type=jnp.float32,
    )
    readout_wide = readout_weight.astype(jnp.float32)
    grad_hidden = (
        residual_slope[0][:, None] * readout_wide[0][None, :]
        + residual_slope[1][:, None] * readout_wide[1][None, :]
    )
    grad_update = jnp.zeros((features, features), jnp.float32)
    grad_node_bias = jnp.zeros((features,), jnp.float32)
    grad_edge_bias = jnp.zeros((features,), jnp.float32)
    state_list, pair_list, input_list, lower_list = ([], [], [], [])
    for (
        flat_hidden,
        query_part,
        key_part,
        key_near,
        query_kept,
        flat_message,
        before,
        update,
    ) in reversed(saved):
        down_rows = grad_hidden.astype(jnp.bfloat16)
        grad_update = grad_update + contract_rows(update, down_rows)
        grad_before = times_transpose(down_rows, update_weight) * silu_slope(before)
        grad_node_bias = grad_node_bias + jnp.sum(grad_before, axis=0)
        lower_rows = grad_before.astype(jnp.bfloat16)
        grad_inputs = times_transpose(lower_rows, node_weight)
        sending = (
            grad_inputs[:, features:].reshape(samples, height, width, features) / degree
        ).astype(jnp.bfloat16)
        stacked = jnp.concatenate([query_part, sending], axis=-1)
        padded_pair, distant_pair = fetch_pair(stacked, span)
        pair_near = arrange(padded_pair, distant_pair, height, width)
        query_near = [piece_pair[..., :features] for piece_pair in pair_near]
        sending_near = [piece_pair[..., features:] for piece_pair in pair_near]
        sending_wide = sending.astype(jnp.float32)
        query_wide = query_part.astype(jnp.float32)
        key_wide = key_part.astype(jnp.float32)
        grad_query = jnp.zeros((samples, height, width, features), jnp.float32)
        grad_key = jnp.zeros((samples, height, width, features), jnp.float32)
        for inside, key_other, query_other, sending_other in zip(
            masks, key_near, query_near, sending_near
        ):
            grad_query = grad_query + inside * sending_wide * silu_slope(
                query_wide + key_other.astype(jnp.float32) + edge_bias
            )
            grad_key = grad_key + inside * sending_other.astype(jnp.float32) * silu_slope(
                query_other.astype(jnp.float32) + key_wide + edge_bias
            )
        grad_edge_bias = grad_edge_bias + jnp.sum(grad_query, axis=(0, 1, 2))
        pair_rows = (
            jnp.concatenate([grad_query, grad_key], axis=-1)
            .astype(jnp.bfloat16)
            .reshape(points, 2 * features)
        )
        grad_hidden = (
            grad_hidden + grad_inputs[:, :features] + times_transpose(pair_rows, pair_weight)
        )
        state_list.append(flat_hidden)
        pair_list.append(pair_rows)
        input_list.append(jnp.concatenate([flat_hidden, flat_message], axis=1))
        lower_list.append(lower_rows)
    grad_zero = grad_hidden.reshape(samples, height, width, features)
    point_gradient = grad_zero * math.sqrt(total_points)
    grad_gain = jnp.sum(grad_zero * normed, axis=(0, 1, 2))
    grad_table = lax.dot_general(
        onehot,
        grad_hidden,
        (((0,), (0,)), ((), ())),
        precision=HIGHEST,
        preferred_element_type=jnp.float32,
    )
    scaled = grad_zero * norm_gain
    power_gradient = inverse * (scaled - normed * jnp.mean(scaled * normed, axis=-1, keepdims=True))

    def beam_update_step(running, inputs):
        covariance_block, weight_rows = inputs
        projected_beams = jnp.dot(
            covariance_block, encoder_beam_weight, preferred_element_type=jnp.float32
        ).reshape(width, antennas, features)
        return (running + jnp.sum(projected_beams * weight_rows[:, None, :], axis=0), None)

    beam_gradient, ignored_value = lax.scan(
        beam_update_step,
        jnp.zeros((antennas, features), jnp.float32),
        (block_list, power_gradient.reshape(samples * height, width, features)),
    )
    beam_gradient = 2.0 * beam_gradient
    small_sums = lax.psum(
        (
            grad_update,
            beam_gradient,
            grad_edge_bias,
            grad_node_bias,
            grad_gain,
            grad_table,
            grad_readout,
        ),
        ("gx", "gy"),
    )
    rows_state = jnp.concatenate(state_list, axis=0)
    rows_pair = jnp.concatenate(pair_list, axis=0)
    rows_input = jnp.concatenate(input_list, axis=0)
    rows_lower = jnp.concatenate(lower_list, axis=0)
    sliced = rows_state
    pair_part = lax.psum_scatter(
        contract_rows(sliced, rows_pair), "gx", scatter_dimension=0, tiled=True
    )
    sliced = rows_input
    node_part = lax.psum_scatter(
        contract_rows(sliced, rows_lower), "gx", scatter_dimension=0, tiled=True
    )
    grad_pair_weight, grad_node_weight = lax.psum((pair_part, node_part), "gy")
    return (
        estimates.reshape(2, samples, height, width),
        grad_pair_weight,
        grad_node_weight,
        small_sums[0],
        small_sums[1],
        small_sums[2],
        small_sums[3],
        small_sums[4],
        small_sums[5],
        small_sums[6],
        point_gradient,
    )


def solution(mesh):
    in_specs = (
        P(None, "gx", "gy", None),
        P(None, "gx", "gy"),
        P(None, None, "gx", "gy"),
        P(),
        P(),
        P(),
        P(),
        P(),
        P(),
        P(),
        P(),
        P(),
    )
    out_specs = (
        P(None, None, "gx", "gy"),
        P("gx", None),
        P("gx", None),
        P(),
        P(),
        P(),
        P(),
        P(),
        P(),
        P(),
        P(None, "gx", "gy", None),
    )
    return jax.shard_map(
        on_device, mesh=mesh, in_specs=in_specs, out_specs=out_specs, check_vma=False
    )
```

profile of v0, /device:TPU:0, one launch (start us, length us, event | category | flops | bytes accessed | tf_op | source)
XLA Modules:
  0.0 417.7 jit_solution(15946256082281819394)
XLA Ops:
  13.3 19.8 %while.21 = (s32[]{:T(128)}, f32[16,8,512]{2,1,0:T(8,128)S(1)}, bf16[16,512,64]{2,1,0:T(8,128)(2,1)}, bf16[64,512]{1,0:T(8,128)(2,1)S(1)}, f32[64,512]{1,0:T(8,128)S(1)}, /*index=5*/s32[]{:T(128)}) while((s32[]{:T(128)}, f32[16,8,512]{2,1,0:T(8,128)S(1)}, bf16[16,512,64]{2,1,0:T(8,128)(2,1)}, bf16[64,512]{1,0:T(8,128)(2,1)S(1)}, ...), condition=%wide.region_2.3_spmd, body=%wide.region_0.2_spmd.sunk | while | flops 34074624 | bytes 442453 | solution.py:130
  34.7 5.6 %collective-permute-start.5 = (bf16[4,4,8,512]{3,2,1,0:T(8,128)(2,1)S(1)}, bf16[4,4,8,512]{3,2,1,0:T(8,128)(2,1)}, u32[]{:S(2)}, u32[]{:S(2)}) collective-permute-start(bf16[4,4,8,512]{3,2,1,0:T(8,128)(2,1)S(1)} %get-tuple-element.147), channel_id=1, source_target_pairs={{0,8},{4,12},{8,16},{12,20},{16,24},{20,28},{1,9},{5,13},{9,17},{1... | collective-permute-start | bytes 393224 | tf_op jit(solution)/shard_map/ppermute | solution.py:36
  43.0 4.5 %collective-permute-start = (bf16[4,1,8,512]{3,2,1,0:T(8,128)(2,1)S(1)}, bf16[4,1,8,512]{3,2,1,0:T(8,128)(2,1)S(1)}, u32[]{:S(2)}, u32[]{:S(2)}) collective-permute-start(bf16[4,1,8,512]{3,2,1,0:T(8,128)(2,1)S(1)} %get-tuple-element.160), channel_id=1, source_target_pairs={{0,4},{4,8},{8,12},{12,16},{16,20},{20,24},{24,28},{1,5},{5,9},{9,... | collective-permute-start | bytes 98312 | tf_op jit(solution)/shard_map/ppermute | solution.py:24
  61.5 4.9 %collective-permute-start.6 = (bf16[4,1,8,512]{3,2,1,0:T(8,128)(2,1)S(1)}, bf16[4,1,8,512]{3,2,1,0:T(8,128)(2,1)S(1)}, u32[]{:S(2)}, u32[]{:S(2)}) collective-permute-start(bf16[4,1,8,512]{3,2,1,0:T(8,128)(2,1)S(1)} %get-tuple-element.158), channel_id=1, source_target_pairs={{0,4},{4,8},{8,12},{12,16},{16,20},{20,24},{24,28},{1,5},{5,9},{9,... | collective-permute-start | bytes 98312 | tf_op jit(solution)/shard_map/ppermute | solution.py:24
  73.5 6.6 %collective-permute-start.11 = (bf16[4,4,8,512]{3,2,1,0:T(8,128)(2,1)S(1)}, bf16[4,4,8,512]{3,2,1,0:T(8,128)(2,1)S(1)}, u32[]{:S(2)}, u32[]{:S(2)}) collective-permute-start(bf16[4,4,8,512]{3,2,1,0:T(8,128)(2,1)S(1)} %get-tuple-element.151), channel_id=1, source_target_pairs={{0,8},{4,12},{8,16},{12,20},{16,24},{20,28},{1,9},{5,13},{9,17},{1... | collective-permute-start | bytes 393224 | tf_op jit(solution)/shard_map/ppermute | solution.py:36
  83.2 5.0 %collective-permute-done.10 = bf16[4,4,8,512]{3,2,1,0:T(8,128)(2,1)S(1)} collective-permute-done((bf16[4,4,8,512]{3,2,1,0:T(8,128)(2,1)S(1)}, bf16[4,4,8,512]{3,2,1,0:T(8,128)(2,1)S(1)}, u32[]{:S(2)}, u32[]{:S(2)}) %collective-permute-start.10) | collective-permute-done | bytes 131104 | tf_op jit(solution)/shard_map/ppermute | solution.py:36
  91.4 4.5 %collective-permute-start.12 = (bf16[4,1,8,512]{3,2,1,0:T(8,128)(2,1)S(1)}, bf16[4,1,8,512]{3,2,1,0:T(8,128)(2,1)S(1)}, u32[]{:S(2)}, u32[]{:S(2)}) collective-permute-start(bf16[4,1,8,512]{3,2,1,0:T(8,128)(2,1)S(1)} %get-tuple-element.156), channel_id=1, source_target_pairs={{0,4},{4,8},{8,12},{12,16},{16,20},{20,24},{24,28},{1,5},{5,9},{9,... | collective-permute-start | bytes 98312 | tf_op jit(solution)/shard_map/ppermute | solution.py:24
  100.4 5.4 %collective-permute-start.17 = (bf16[4,4,8,512]{3,2,1,0:T(8,128)(2,1)S(1)}, bf16[4,4,8,512]{3,2,1,0:T(8,128)(2,1)S(1)}, u32[]{:S(2)}, u32[]{:S(2)}) collective-permute-start(bf16[4,4,8,512]{3,2,1,0:T(8,128)(2,1)S(1)} %get-tuple-element.155), channel_id=1, source_target_pairs={{0,8},{4,12},{8,16},{12,20},{16,24},{20,28},{1,9},{5,13},{9,17},{1... | collective-permute-start | bytes 393224 | tf_op jit(solution)/shard_map/ppermute | solution.py:36
  108.3 4.4 %collective-permute-done.16 = bf16[4,4,8,512]{3,2,1,0:T(8,128)(2,1)S(1)} collective-permute-done((bf16[4,4,8,512]{3,2,1,0:T(8,128)(2,1)S(1)}, bf16[4,4,8,512]{3,2,1,0:T(8,128)(2,1)S(1)}, u32[]{:S(2)}, u32[]{:S(2)}) %collective-permute-start.16) | collective-permute-done | bytes 131104 | tf_op jit(solution)/shard_map/ppermute | solution.py:36
  119.7 4.5 %collective-permute-start.18 = (bf16[4,1,8,1024]{3,2,1,0:T(8,128)(2,1)S(1)}, bf16[4,1,8,1024]{3,2,1,0:T(8,128)(2,1)S(1)}, u32[]{:S(2)}, u32[]{:S(2)}) collective-permute-start(bf16[4,1,8,1024]{3,2,1,0:T(8,128)(2,1)S(1)} %get-tuple-element.152), channel_id=1, source_target_pairs={{0,4},{4,8},{8,12},{12,16},{16,20},{20,24},{24,28},{1,5},{5,9},{9,... | collective-permute-start | bytes 196616 | tf_op jit(solution)/shard_map/ppermute | solution.py:24
  135.0 5.4 %collective-permute-done.21 = bf16[4,6,1,1024]{3,2,1,0:T(2,128)(2,1)S(1)} collective-permute-done((bf16[4,6,1,1024]{3,2,1,0:T(2,128)(2,1)S(1)}, bf16[4,6,1,1024]{3,2,1,0:T(2,128)(2,1)S(1)}, u32[]{:S(2)}, u32[]{:S(2)}) %collective-permute-start.21) | collective-permute-done | bytes 49184 | tf_op jit(solution)/shard_map/ppermute | solution.py:26
  147.6 4.5 %collective-permute-start.24 = (bf16[4,1,8,1024]{3,2,1,0:T(8,128)(2,1)S(1)}, bf16[4,1,8,1024]{3,2,1,0:T(8,128)(2,1)S(1)}, u32[]{:S(2)}, u32[]{:S(2)}) collective-permute-start(bf16[4,1,8,1024]{3,2,1,0:T(8,128)(2,1)S(1)} %get-tuple-element.148), channel_id=1, source_target_pairs={{0,4},{4,8},{8,12},{12,16},{16,20},{20,24},{24,28},{1,5},{5,9},{9,... | collective-permute-start | bytes 196616 | tf_op jit(solution)/shard_map/ppermute | solution.py:24
  152.1 4.6 %collective-permute-start.29 = (bf16[4,4,8,1024]{3,2,1,0:T(8,128)(2,1)S(1)}, bf16[4,4,8,1024]{3,2,1,0:T(8,128)(2,1)S(1)}, u32[]{:S(2)}, u32[]{:S(2)}) collective-permute-start(bf16[4,4,8,1024]{3,2,1,0:T(8,128)(2,1)S(1)} %pad_maximum_fusion.7), channel_id=1, source_target_pairs={{0,8},{4,12},{8,16},{12,20},{16,24},{20,28},{1,9},{5,13},{9,17},{1... | collective-permute-start | bytes 786440 | tf_op jit(solution)/shard_map/ppermute | solution.py:36
  158.2 4.3 %collective-permute-start.26 = (bf16[4,6,1,1024]{3,2,1,0:T(2,128)(2,1)S(1)}, bf16[4,6,1,1024]{3,2,1,0:T(2,128)(2,1)S(1)}, u32[]{:S(2)}, u32[]{:S(2)}) collective-permute-start(bf16[4,6,1,1024]{3,2,1,0:T(2,128)(2,1)S(1)} %get-tuple-element.131), channel_id=1, source_target_pairs={{0,1},{1,2},{2,3},{4,5},{5,6},{6,7},{8,9},{9,10},{10,11},{12,13},{... | collective-permute-start | bytes 147464 | tf_op jit(solution)/shard_map/ppermute | solution.py:24
  180.1 4.5 %collective-permute-start.30 = (bf16[4,1,8,1024]{3,2,1,0:T(8,128)(2,1)S(1)}, bf16[4,1,8,1024]{3,2,1,0:T(8,128)(2,1)S(1)}, u32[]{:S(2)}, u32[]{:S(2)}) collective-permute-start(bf16[4,1,8,1024]{3,2,1,0:T(8,128)(2,1)S(1)} %get-tuple-element.144), channel_id=1, source_target_pairs={{0,4},{4,8},{8,12},{12,16},{16,20},{20,24},{24,28},{1,5},{5,9},{9,... | collective-permute-start | bytes 196616 | tf_op jit(solution)/shard_map/ppermute | solution.py:24
  184.7 4.6 %collective-permute-start.35 = (bf16[4,4,8,1024]{3,2,1,0:T(8,128)(2,1)S(1)}, bf16[4,4,8,1024]{3,2,1,0:T(8,128)(2,1)S(1)}, u32[]{:S(2)}, u32[]{:S(2)}) collective-permute-start(bf16[4,4,8,1024]{3,2,1,0:T(8,128)(2,1)S(1)} %pad_maximum_fusion.8), channel_id=1, source_target_pairs={{0,8},{4,12},{8,16},{12,20},{16,24},{20,28},{1,9},{5,13},{9,17},{1... | collective-permute-start | bytes 786440 | tf_op jit(solution)/shard_map/ppermute | solution.py:36
  190.7 4.3 %collective-permute-start.32 = (bf16[4,6,1,1024]{3,2,1,0:T(2,128)(2,1)S(1)}, bf16[4,6,1,1024]{3,2,1,0:T(2,128)(2,1)S(1)}, u32[]{:S(2)}, u32[]{:S(2)}) collective-permute-start(bf16[4,6,1,1024]{3,2,1,0:T(2,128)(2,1)S(1)} %get-tuple-element.127), channel_id=1, source_target_pairs={{0,1},{1,2},{2,3},{4,5},{5,6},{6,7},{8,9},{9,10},{10,11},{12,13},{... | collective-permute-start | bytes 147464 | tf_op jit(solution)/shard_map/ppermute | solution.py:24
  199.1 8.5 %collective-permute-done.34 = bf16[4,4,8,1024]{3,2,1,0:T(8,128)(2,1)S(1)} collective-permute-done((bf16[4,4,8,1024]{3,2,1,0:T(8,128)(2,1)S(1)}, bf16[4,4,8,1024]{3,2,1,0:T(8,128)(2,1)S(1)}, u32[]{:S(2)}, u32[]{:S(2)}) %collective-permute-start.34) | collective-permute-done | bytes 262176 | tf_op jit(solution)/shard_map/ppermute | solution.py:36
  213.5 20.6 %while.22 = (s32[]{:T(128)}, f32[64,512]{1,0:T(8,128)S(1)}, bf16[16,512,64]{2,1,0:T(8,128)(2,1)}, bf16[64,512]{1,0:T(8,128)(2,1)S(1)}, f32[16,8,512]{2,1,0:T(8,128)S(1)}, /*index=5*/s32[]{:T(128)}, s32[]{:T(128)}) while((s32[]{:T(128)}, f32[64,512]{1,0:T(8,128)S(1)}, bf16[16,512,64]{2,1,0:T(8,128)(2,1)}, ...), condition=%wide.region_12.13_spmd.clone, body=%wide.region_10.12_spmd.clone.sunk | while | flops 34111488 | bytes 835687 | solution.py:264
  235.9 10.6 %reduce-scatter.5.cloned.1.call-done = f32[128,512]{1,0:T(8,128)} async-done(((f32[1024,512]{1,0:T(8,128)}), f32[128,512]{1,0:T(8,128)}) %reduce-scatter.5.cloned.1.call-update) | async-done | bytes 262160 | tf_op jit(solution)/shard_map/reduce_scatter | solution.py:291
  246.5 71.5 %reduce-scatter.3.cloned.1.call-done = f32[64,1024]{1,0:T(8,128)} async-done(((f32[512,1024]{1,0:T(8,128)}), f32[64,1024]{1,0:T(8,128)}) %reduce-scatter.3.cloned.1.call-update) | async-done | bytes 262160 | tf_op jit(solution)/shard_map/reduce_scatter | solution.py:287
  318.4 40.7 %all-reduce = (f32[512]{0:T(512)}, f32[512]{0:T(512)}, f32[512]{0:T(512)}, f32[16,512]{1,0:T(8,128)}, f32[2,512]{1,0:T(2,128)}) all-reduce(f32[512]{0:T(512)S(1)} %add_add_fusion.1, f32[512]{0:T(512)S(1)} %add_add_fusion, f32[512]{0:T(512)S(1)} %get-tuple-element.85, ...), channel_id=1, replica_groups=mesh['gx'=8,'gy'=4] {'gx','gy'}, use_global_device_ids=true, to_apply=%region_17.18 | all-reduce | flops 10752 | bytes 86016 | tf_op jit(solution)/shard_map/psum | solution.py:270
  359.0 11.6 %all-reduce.6.cloned.1.call-done = (f32[512,512]{1,0:T(8,128)}, f32[64,512]{1,0:T(8,128)}) async-done(((f32[512,512]{1,0:T(8,128)}, f32[64,512]{1,0:T(8,128)}), (f32[512,512]{1,0:T(8,128)}, f32[64,512]{1,0:T(8,128)})) %all-reduce.6.cloned.1.call-update) | async-done | bytes 1179664 | tf_op jit(solution)/shard_map/psum | solution.py:270
  370.6 34.7 %all-reduce.8.cloned.1.call-done = (f32[64,1024]{1,0:T(8,128)}, f32[128,512]{1,0:T(8,128)}) async-done(((f32[64,1024]{1,0:T(8,128)}, f32[128,512]{1,0:T(8,128)}), (f32[64,1024]{1,0:T(8,128)}, f32[128,512]{1,0:T(8,128)})) %all-reduce.8.cloned.1.call-update) | async-done | bytes 524304 | tf_op jit(solution)/shard_map/psum | solution.py:294
  (434 shorter events, 143.7 us)
Async XLA Ops:
  8.0 238.5 %reduce-scatter.5.cloned.1.call-start = ((), (), s32[]{:S(2)}) async-start(), calls=%async_computation.3 | async-start | bytes 2359296 | tf_op jit(solution)/shard_map/reduce_scatter | solution.py:291
  34.7 21.7 %collective-permute-start.5 = (bf16[4,4,8,512]{3,2,1,0:T(8,128)(2,1)S(1)}, bf16[4,4,8,512]{3,2,1,0:T(8,128)(2,1)}, u32[]{:S(2)}, u32[]{:S(2)}) collective-permute-start(bf16[4,4,8,512]{3,2,1,0:T(8,128)(2,1)S(1)} %get-tuple-element.147), channel_id=1, source_target_pairs={{0,8},{4,12},{8,16},{12,20},{16,24},{20,28},{1,9},{5,13},{9,17},{1... | collective-permute-start | bytes 393224 | tf_op jit(solution)/shard_map/ppermute | solution.py:36
  40.4 16.1 %collective-permute-start.4 = (bf16[4,4,8,512]{3,2,1,0:T(8,128)(2,1)S(1)}, bf16[4,4,8,512]{3,2,1,0:T(8,128)(2,1)}, u32[]{:S(2)}, u32[]{:S(2)}) collective-permute-start(bf16[4,4,8,512]{3,2,1,0:T(8,128)(2,1)S(1)} %get-tuple-element.147), channel_id=1, source_target_pairs={{8,0},{12,4},{16,8},{20,12},{24,16},{28,20},{9,1},{13,5},{17,9},{2... | collective-permute-start | bytes 393224 | tf_op jit(solution)/shard_map/ppermute | solution.py:36
  68.1 13.3 %collective-permute-start.8 = (bf16[4,6,1,512]{3,2,1,0:T(2,128)(2,1)S(1)}, bf16[4,6,1,512]{3,2,1,0:T(2,128)(2,1)S(1)}, u32[]{:S(2)}, u32[]{:S(2)}) collective-permute-start(bf16[4,6,1,512]{3,2,1,0:T(2,128)(2,1)S(1)} %get-tuple-element.168), channel_id=1, source_target_pairs={{0,1},{1,2},{2,3},{4,5},{5,6},{6,7},{8,9},{9,10},{10,11},{12,13},{... | collective-permute-start | bytes 73736 | tf_op jit(solution)/shard_map/ppermute | solution.py:24
  71.9 9.4 %collective-permute-start.9 = (bf16[4,6,1,512]{3,2,1,0:T(2,128)(2,1)S(1)}, bf16[4,6,1,512]{3,2,1,0:T(2,128)(2,1)S(1)}, u32[]{:S(2)}, u32[]{:S(2)}) collective-permute-start(bf16[4,6,1,512]{3,2,1,0:T(2,128)(2,1)S(1)} %get-tuple-element.169), channel_id=1, source_target_pairs={{1,0},{2,1},{3,2},{5,4},{6,5},{7,6},{9,8},{10,9},{11,10},{13,12},{... | collective-permute-start | bytes 73736 | tf_op jit(solution)/shard_map/ppermute | solution.py:26
  73.5 9.8 %collective-permute-start.11 = (bf16[4,4,8,512]{3,2,1,0:T(8,128)(2,1)S(1)}, bf16[4,4,8,512]{3,2,1,0:T(8,128)(2,1)S(1)}, u32[]{:S(2)}, u32[]{:S(2)}) collective-permute-start(bf16[4,4,8,512]{3,2,1,0:T(8,128)(2,1)S(1)} %get-tuple-element.151), channel_id=1, source_target_pairs={{0,8},{4,12},{8,16},{12,20},{16,24},{20,28},{1,9},{5,13},{9,17},{1... | collective-permute-start | bytes 393224 | tf_op jit(solution)/shard_map/ppermute | solution.py:36
  80.0 8.2 %collective-permute-start.10 = (bf16[4,4,8,512]{3,2,1,0:T(8,128)(2,1)S(1)}, bf16[4,4,8,512]{3,2,1,0:T(8,128)(2,1)S(1)}, u32[]{:S(2)}, u32[]{:S(2)}) collective-permute-start(bf16[4,4,8,512]{3,2,1,0:T(8,128)(2,1)S(1)} %get-tuple-element.151), channel_id=1, source_target_pairs={{8,0},{12,4},{16,8},{20,12},{24,16},{28,20},{9,1},{13,5},{17,9},{2... | collective-permute-start | bytes 393224 | tf_op jit(solution)/shard_map/ppermute | solution.py:36
  97.6 9.5 %collective-permute-start.14 = (bf16[4,6,1,512]{3,2,1,0:T(2,128)(2,1)S(1)}, bf16[4,6,1,512]{3,2,1,0:T(2,128)(2,1)S(1)}, u32[]{:S(2)}, u32[]{:S(2)}) collective-permute-start(bf16[4,6,1,512]{3,2,1,0:T(2,128)(2,1)S(1)} %get-tuple-element.164), channel_id=1, source_target_pairs={{0,1},{1,2},{2,3},{4,5},{5,6},{6,7},{8,9},{9,10},{10,11},{12,13},{... | collective-permute-start | bytes 73736 | tf_op jit(solution)/shard_map/ppermute | solution.py:24
  98.9 8.3 %collective-permute-start.15 = (bf16[4,6,1,512]{3,2,1,0:T(2,128)(2,1)S(1)}, bf16[4,6,1,512]{3,2,1,0:T(2,128)(2,1)S(1)}, u32[]{:S(2)}, u32[]{:S(2)}) collective-permute-start(bf16[4,6,1,512]{3,2,1,0:T(2,128)(2,1)S(1)} %get-tuple-element.165), channel_id=1, source_target_pairs={{1,0},{2,1},{3,2},{5,4},{6,5},{7,6},{9,8},{10,9},{11,10},{13,12},{... | collective-permute-start | bytes 73736 | tf_op jit(solution)/shard_map/ppermute | solution.py:26
  118.4 11.3 %collective-permute-start.19 = (bf16[4,1,8,1024]{3,2,1,0:T(8,128)(2,1)S(1)}, bf16[4,1,8,1024]{3,2,1,0:T(8,128)(2,1)S(1)}, u32[]{:S(2)}, u32[]{:S(2)}) collective-permute-start(bf16[4,1,8,1024]{3,2,1,0:T(8,128)(2,1)S(1)} %get-tuple-element.153), channel_id=1, source_target_pairs={{4,0},{8,4},{12,8},{16,12},{20,16},{24,20},{28,24},{5,1},{9,5},{13... | collective-permute-start | bytes 196616 | tf_op jit(solution)/shard_map/ppermute | solution.py:26
  119.7 10.0 %collective-permute-start.18 = (bf16[4,1,8,1024]{3,2,1,0:T(8,128)(2,1)S(1)}, bf16[4,1,8,1024]{3,2,1,0:T(8,128)(2,1)S(1)}, u32[]{:S(2)}, u32[]{:S(2)}) collective-permute-start(bf16[4,1,8,1024]{3,2,1,0:T(8,128)(2,1)S(1)} %get-tuple-element.152), channel_id=1, source_target_pairs={{0,4},{4,8},{8,12},{12,16},{16,20},{20,24},{24,28},{1,5},{5,9},{9,... | collective-permute-start | bytes 196616 | tf_op jit(solution)/shard_map/ppermute | solution.py:24
  124.3 16.5 %collective-permute-start.23 = (bf16[4,4,8,1024]{3,2,1,0:T(8,128)(2,1)S(1)}, bf16[4,4,8,1024]{3,2,1,0:T(8,128)(2,1)S(1)}, u32[]{:S(2)}, u32[]{:S(2)}) collective-permute-start(bf16[4,4,8,1024]{3,2,1,0:T(8,128)(2,1)S(1)} %pad_maximum_fusion.6), channel_id=1, source_target_pairs={{0,8},{4,12},{8,16},{12,20},{16,24},{20,28},{1,9},{5,13},{9,17},{1... | collective-permute-start | bytes 786440 | tf_op jit(solution)/shard_map/ppermute | solution.py:36
  128.3 12.6 %collective-permute-start.22 = (bf16[4,4,8,1024]{3,2,1,0:T(8,128)(2,1)S(1)}, bf16[4,4,8,1024]{3,2,1,0:T(8,128)(2,1)S(1)}, u32[]{:S(2)}, u32[]{:S(2)}) collective-permute-start(bf16[4,4,8,1024]{3,2,1,0:T(8,128)(2,1)S(1)} %pad_maximum_fusion.6), channel_id=1, source_target_pairs={{8,0},{12,4},{16,8},{20,12},{24,16},{28,20},{9,1},{13,5},{17,9},{2... | collective-permute-start | bytes 786440 | tf_op jit(solution)/shard_map/ppermute | solution.py:36
  146.3 11.8 %collective-permute-start.25 = (bf16[4,1,8,1024]{3,2,1,0:T(8,128)(2,1)S(1)}, bf16[4,1,8,1024]{3,2,1,0:T(8,128)(2,1)S(1)}, u32[]{:S(2)}, u32[]{:S(2)}) collective-permute-start(bf16[4,1,8,1024]{3,2,1,0:T(8,128)(2,1)S(1)} %get-tuple-element.149), channel_id=1, source_target_pairs={{4,0},{8,4},{12,8},{16,12},{20,16},{24,20},{28,24},{5,1},{9,5},{13... | collective-permute-start | bytes 196616 | tf_op jit(solution)/shard_map/ppermute | solution.py:26
  147.6 10.5 %collective-permute-start.24 = (bf16[4,1,8,1024]{3,2,1,0:T(8,128)(2,1)S(1)}, bf16[4,1,8,1024]{3,2,1,0:T(8,128)(2,1)S(1)}, u32[]{:S(2)}, u32[]{:S(2)}) collective-permute-start(bf16[4,1,8,1024]{3,2,1,0:T(8,128)(2,1)S(1)} %get-tuple-element.148), channel_id=1, source_target_pairs={{0,4},{4,8},{8,12},{12,16},{16,20},{20,24},{24,28},{1,5},{5,9},{9,... | collective-permute-start | bytes 196616 | tf_op jit(solution)/shard_map/ppermute | solution.py:24
  152.1 14.2 %collective-permute-start.29 = (bf16[4,4,8,1024]{3,2,1,0:T(8,128)(2,1)S(1)}, bf16[4,4,8,1024]{3,2,1,0:T(8,128)(2,1)S(1)}, u32[]{:S(2)}, u32[]{:S(2)}) collective-permute-start(bf16[4,4,8,1024]{3,2,1,0:T(8,128)(2,1)S(1)} %pad_maximum_fusion.7), channel_id=1, source_target_pairs={{0,8},{4,12},{8,16},{12,20},{16,24},{20,28},{1,9},{5,13},{9,17},{1... | collective-permute-start | bytes 786440 | tf_op jit(solution)/shard_map/ppermute | solution.py:36
  156.7 9.7 %collective-permute-start.28 = (bf16[4,4,8,1024]{3,2,1,0:T(8,128)(2,1)S(1)}, bf16[4,4,8,1024]{3,2,1,0:T(8,128)(2,1)S(1)}, u32[]{:S(2)}, u32[]{:S(2)}) collective-permute-start(bf16[4,4,8,1024]{3,2,1,0:T(8,128)(2,1)S(1)} %pad_maximum_fusion.7), channel_id=1, source_target_pairs={{8,0},{12,4},{16,8},{20,12},{24,16},{28,20},{9,1},{13,5},{17,9},{2... | collective-permute-start | bytes 786440 | tf_op jit(solution)/shard_map/ppermute | solution.py:36
  172.9 145.1 %reduce-scatter.3.cloned.1.call-start = ((), (), s32[]{:S(2)}) async-start(), calls=%async_computation.2 | async-start | bytes 2359296 | tf_op jit(solution)/shard_map/reduce_scatter | solution.py:287
  178.8 11.8 %collective-permute-start.31 = (bf16[4,1,8,1024]{3,2,1,0:T(8,128)(2,1)S(1)}, bf16[4,1,8,1024]{3,2,1,0:T(8,128)(2,1)S(1)}, u32[]{:S(2)}, u32[]{:S(2)}) collective-permute-start(bf16[4,1,8,1024]{3,2,1,0:T(8,128)(2,1)S(1)} %get-tuple-element.145), channel_id=1, source_target_pairs={{4,0},{8,4},{12,8},{16,12},{20,16},{24,20},{28,24},{5,1},{9,5},{13... | collective-permute-start | bytes 196616 | tf_op jit(solution)/shard_map/ppermute | solution.py:26
  180.1 10.5 %collective-permute-start.30 = (bf16[4,1,8,1024]{3,2,1,0:T(8,128)(2,1)S(1)}, bf16[4,1,8,1024]{3,2,1,0:T(8,128)(2,1)S(1)}, u32[]{:S(2)}, u32[]{:S(2)}) collective-permute-start(bf16[4,1,8,1024]{3,2,1,0:T(8,128)(2,1)S(1)} %get-tuple-element.144), channel_id=1, source_target_pairs={{0,4},{4,8},{8,12},{12,16},{16,20},{20,24},{24,28},{1,5},{5,9},{9,... | collective-permute-start | bytes 196616 | tf_op jit(solution)/shard_map/ppermute | solution.py:24
  184.7 14.5 %collective-permute-start.35 = (bf16[4,4,8,1024]{3,2,1,0:T(8,128)(2,1)S(1)}, bf16[4,4,8,1024]{3,2,1,0:T(8,128)(2,1)S(1)}, u32[]{:S(2)}, u32[]{:S(2)}) collective-permute-start(bf16[4,4,8,1024]{3,2,1,0:T(8,128)(2,1)S(1)} %pad_maximum_fusion.8), channel_id=1, source_target_pairs={{0,8},{4,12},{8,16},{12,20},{16,24},{20,28},{1,9},{5,13},{9,17},{1... | collective-permute-start | bytes 786440 | tf_op jit(solution)/shard_map/ppermute | solution.py:36
  189.3 18.4 %collective-permute-start.34 = (bf16[4,4,8,1024]{3,2,1,0:T(8,128)(2,1)S(1)}, bf16[4,4,8,1024]{3,2,1,0:T(8,128)(2,1)S(1)}, u32[]{:S(2)}, u32[]{:S(2)}) collective-permute-start(bf16[4,4,8,1024]{3,2,1,0:T(8,128)(2,1)S(1)} %pad_maximum_fusion.8), channel_id=1, source_target_pairs={{8,0},{12,4},{16,8},{20,12},{24,16},{28,20},{9,1},{13,5},{17,9},{2... | collective-permute-start | bytes 786440 | tf_op jit(solution)/shard_map/ppermute | solution.py:36
  212.7 157.9 %all-reduce.6.cloned.1.call-start = ((), (), s32[]{:S(2)}) async-start(), calls=%async_computation.4 | async-start | bytes 2359296 | tf_op jit(solution)/shard_map/psum | solution.py:270
  234.9 170.4 %all-reduce.8.cloned.1.call-start = ((), (), s32[]{:S(2)}) async-start(), calls=%async_computation.5 | async-start | bytes 1048576 | tf_op jit(solution)/shard_map/psum | solution.py:294
  (99 other events, 2151.2 us)
Sparse Core Ops, SparseCore 0:
  173.0 73.4 reduce-scatter.4
  250.0 67.9 reduce-scatter.2
Sparse Core Ops, SparseCore 1:
  235.0 135.6 all-reduce.5
  372.9 32.3 all-reduce.7
where the time goes:
time: 420 us; the launch traced here: 418 us
  waiting for transfers between devices  162 us (39%)
  starting transfers between devices  102 us (24%)
  local copies, waits for them, and re-layouts  45 us (11%)
  blocking collectives  40.7 us (10%)
  matrix products  28.8 us (7%)
  other arithmetic  20.5 us (5%)
  between operations  17.4 us (4%)
    reduce_scatter x1, waiting for transfers between devices, on_device(): lax.psum_scatter(contract_rows(sliced, rows_pair), 'gx', scatter_dimensio...  71.5 us
    ppermute x12, starting transfers between devices, with_halo(): lax.ppermute(tail, axis, [(i, (i + 1) % count) for i in range(ends)])  47.1 us
    psum x1, blocking collectives, on_device(): lax.psum((grad_update, beam_gradient, grad_edge_bias, grad_node_bias, gra...  40.7 us
    ppermute x12, starting transfers between devices, from_behind(): lax.ppermute(value, axis, [(source, source + steps) for source in range(l...  38.6 us
    psum x1, waiting for transfers between devices, on_device(): grad_pair_weight, grad_node_weight = lax.psum((pair_part, node_part), 'gy')  34.7 us
    dynamic_slice x32, local copies, waits for them, and re-layouts, on_device(): lax.map(block_power, block_list).reshape(samples, height, width, features)  29.4 us
    ppermute x12, waiting for transfers between devices, from_behind(): lax.ppermute(value, axis, [(source, source + steps) for source in range(l...  20.7 us
    ppermute x12, starting transfers between devices, with_halo(): lax.ppermute(head, axis, [((i + 1) % count, i) for i in range(ends)])  15.7 us
  transfers between devices with their start and end apart: 40, of which 17 were waited for; matrix products, arithmetic and copies ran while one was open for 9% of the time, Pallas kernels for 0%

commit v1 on v0

--- a/solution.py
+++ b/solution.py
@@ -119,15 +119,14 @@
     for another in masks[1:]:
         degree = degree + another
     beams = encoder_beam_weight.astype(jnp.float32)
-    block_list = covariance.reshape(samples * height, width * antennas, antennas)
-
-    def block_power(covariance_block):
-        projected_beams = jnp.dot(
-            covariance_block, encoder_beam_weight, preferred_element_type=jnp.float32
-        ).reshape(width, antennas, features)
-        return jnp.sum(projected_beams * beams[None], axis=1)
-
-    powers = lax.map(block_power, block_list).reshape(samples, height, width, features)
+    cov_flat = covariance.reshape(points, antennas * antennas)
+    outer = (beams[:, None, :] * beams[None, :, :]).reshape(antennas * antennas, features)
+    outer_hi = outer.astype(jnp.bfloat16)
+    outer_lo = (outer - outer_hi.astype(jnp.float32)).astype(jnp.bfloat16)
+    powers = (
+        jnp.dot(cov_flat, outer_hi, preferred_element_type=jnp.float32)
+        + jnp.dot(cov_flat, outer_lo, preferred_element_type=jnp.float32)
+    ).reshape(samples, height, width, features)
     inverse = lax.rsqrt(jnp.mean(powers * powers, axis=-1, keepdims=True) + EPSILON)
     normed = powers * inverse
     onehot = (pilot_ids.reshape(points, 1) == jnp.arange(pilots, dtype=jnp.int32)[None, :]).astype(
@@ -254,17 +253,12 @@
     scaled = grad_zero * norm_gain
     power_gradient = inverse * (scaled - normed * jnp.mean(scaled * normed, axis=-1, keepdims=True))
 
-    def beam_update_step(running, inputs):
-        covariance_block, weight_rows = inputs
-        projected_beams = jnp.dot(
-            covariance_block, encoder_beam_weight, preferred_element_type=jnp.float32
-        ).reshape(width, antennas, features)
-        return (running + jnp.sum(projected_beams * weight_rows[:, None, :], axis=0), None)
-
-    beam_gradient, ignored_value = lax.scan(
-        beam_update_step,
-        jnp.zeros((antennas, features), jnp.float32),
-        (block_list, power_gradient.reshape(samples * height, width, features)),
+    power_rows = power_gradient.reshape(points, features)
+    power_hi = power_rows.astype(jnp.bfloat16)
+    power_lo = (power_rows - power_hi.astype(jnp.float32)).astype(jnp.bfloat16)
+    spread = contract_rows(cov_flat, power_hi) + contract_rows(cov_flat, power_lo)
+    beam_gradient = jnp.sum(
+        spread.reshape(antennas, antennas, features) * beams[None, :, :], axis=1
     )
     beam_gradient = 2.0 * beam_gradient
     small_sums = lax.psum(

time: 420 us -> 408 us (0.971)
  local copies, waits for them, and re-layouts: 45 us -> 23 us
  other arithmetic: 20.5 us -> 33.7 us
    dynamic_slice x32 -> x0, local copies, waits for them, and re-layouts: 29.4 us -> none  [on_device(): lax.map(block_power, block_list).reshape(samples, height, width, features)]
    ppermute x12, waiting for transfers between devices: 9.93 us -> 19.1 us  [with_halo(): lax.ppermute(head, axis, [((i + 1) % count, i) for i in range(ends)])]
    add x0 -> x1, local copies, waits for them, and re-layouts: none -> 9.06 us  [on_device(): contract_rows(cov_flat, power_hi) + contract_rows(cov_flat, power_lo)]
    dot_general x32 -> x2, matrix products: 8.72 us -> 1.64 us  [the longest x1 0.87 us: on_device(): jnp.dot(cov_flat, outer_lo, preferred_element_type=jnp.float32)]
    dot_general x5 -> x7, matrix products: 7.16 us -> 13.3 us  [contract_rows(): lax.dot_general(left_rows, right_rows, (((0,), (0,)), ((), ())), preferre...]
    ppermute x12, starting transfers between devices: 47.1 us -> 41.8 us  [with_halo(): lax.ppermute(tail, axis, [(i, (i + 1) % count) for i in range(ends)])]
    reduce_sum x1, other arithmetic: 0.1 us -> 4.92 us  [on_device(): jnp.sum(spread.reshape(antennas, antennas, features) * beams[None, :, :],...]
    reshape x1 -> x0, local copies, waits for them, and re-layouts: 4.27 us -> none  [on_device(): covariance.reshape(samples * height, width * antennas, antennas)]
  transfers between devices with their start and end apart: 40 -> 40, of which waited for: 17 -> 17; matrix products, arithmetic and copies ran while one was open for 9% -> 12% of each run, Pallas kernels for 0% -> 0%
where the time goes in v1:
time: 408 us; the launch traced here: 407 us
  waiting for transfers between devices  164 us (40%)
  starting transfers between devices  98.2 us (24%)
  blocking collectives  40.7 us (10%)
  other arithmetic  33.7 us (8%)
  matrix products  29.7 us (7%)
  local copies, waits for them, and re-layouts  23 us (6%)
  between operations  17.3 us (4%)
    reduce_scatter x1, waiting for transfers between devices, on_device(): lax.psum_scatter(contract_rows(sliced, rows_pair), 'gx', scatter_dimensio...  71.3 us
    ppermute x12, starting transfers between devices, with_halo(): lax.ppermute(tail, axis, [(i, (i + 1) % count) for i in range(ends)])  41.8 us
    psum x1, blocking collectives, on_device(): lax.psum((grad_update, beam_gradient, grad_edge_bias, grad_node_bias, gra...  40.7 us
    ppermute x12, starting transfers between devices, from_behind(): lax.ppermute(value, axis, [(source, source + steps) for source in range(l...  40.3 us
    psum x1, waiting for transfers between devices, on_device(): grad_pair_weight, grad_node_weight = lax.psum((pair_part, node_part), 'gy')  34.7 us
    ppermute x12, waiting for transfers between devices, with_halo(): lax.ppermute(head, axis, [((i + 1) % count, i) for i in range(ends)])  19.1 us
    ppermute x12, waiting for transfers between devices, from_behind(): lax.ppermute(value, axis, [(source, source + steps) for source in range(l...  16.8 us
    ppermute x12, starting transfers between devices, with_halo(): lax.ppermute(head, axis, [((i + 1) % count, i) for i in range(ends)])  15.7 us
  transfers between devices with their start and end apart: 40, of which 17 were waited for; matrix products, arithmetic and copies ran while one was open for 12% of the time, Pallas kernels for 0%

profile of v1, /device:TPU:0, one launch (start us, length us, event | category | flops | bytes accessed | tf_op | source)
XLA Modules:
  0.0 406.7 jit_solution(6531887864937461502)
XLA Ops:
  15.2 5.6 %collective-permute-start.5 = (bf16[4,4,8,512]{3,2,1,0:T(8,128)(2,1)}, bf16[4,4,8,512]{3,2,1,0:T(8,128)(2,1)}, u32[]{:S(2)}, u32[]{:S(2)}) collective-permute-start(bf16[4,4,8,512]{3,2,1,0:T(8,128)(2,1)} %get-tuple-element.53), channel_id=1, source_target_pairs={{0,8},{4,12},{8,16},{12,20},{16,24},{20,28},{1,9},{5,13},{9,17},{1... | collective-permute-start | bytes 393224 | tf_op jit(solution)/shard_map/ppermute | solution.py:36
  22.7 4.0 collective-permute-start
  48.1 4.6 %collective-permute-start.6 = (bf16[4,1,8,512]{3,2,1,0:T(8,128)(2,1)S(1)}, bf16[4,1,8,512]{3,2,1,0:T(8,128)(2,1)S(1)}, u32[]{:S(2)}, u32[]{:S(2)}) collective-permute-start(bf16[4,1,8,512]{3,2,1,0:T(8,128)(2,1)S(1)} %get-tuple-element.64), channel_id=1, source_target_pairs={{0,4},{4,8},{8,12},{12,16},{16,20},{20,24},{24,28},{1,5},{5,9},{9,... | collective-permute-start | bytes 98312 | tf_op jit(solution)/shard_map/ppermute | solution.py:24
  54.3 5.1 %collective-permute-done.7 = bf16[4,1,8,512]{3,2,1,0:T(8,128)(2,1)S(1)} collective-permute-done((bf16[4,1,8,512]{3,2,1,0:T(8,128)(2,1)S(1)}, bf16[4,1,8,512]{3,2,1,0:T(8,128)(2,1)S(1)}, u32[]{:S(2)}, u32[]{:S(2)}) %collective-permute-start.7) | collective-permute-done | bytes 32800 | tf_op jit(solution)/shard_map/ppermute | solution.py:26
  70.1 4.4 %collective-permute-done.10 = bf16[4,4,8,512]{3,2,1,0:T(8,128)(2,1)S(1)} collective-permute-done((bf16[4,4,8,512]{3,2,1,0:T(8,128)(2,1)S(1)}, bf16[4,4,8,512]{3,2,1,0:T(8,128)(2,1)S(1)}, u32[]{:S(2)}, u32[]{:S(2)}) %collective-permute-start.10) | collective-permute-done | bytes 131104 | tf_op jit(solution)/shard_map/ppermute | solution.py:36
  76.3 4.5 %collective-permute-start.12 = (bf16[4,1,8,512]{3,2,1,0:T(8,128)(2,1)S(1)}, bf16[4,1,8,512]{3,2,1,0:T(8,128)(2,1)S(1)}, u32[]{:S(2)}, u32[]{:S(2)}) collective-permute-start(bf16[4,1,8,512]{3,2,1,0:T(8,128)(2,1)S(1)} %get-tuple-element.62), channel_id=1, source_target_pairs={{0,4},{4,8},{8,12},{12,16},{16,20},{20,24},{24,28},{1,5},{5,9},{9,... | collective-permute-start | bytes 98312 | tf_op jit(solution)/shard_map/ppermute | solution.py:24
  82.4 4.2 %collective-permute-done.13 = bf16[4,1,8,512]{3,2,1,0:T(8,128)(2,1)S(1)} collective-permute-done((bf16[4,1,8,512]{3,2,1,0:T(8,128)(2,1)S(1)}, bf16[4,1,8,512]{3,2,1,0:T(8,128)(2,1)S(1)}, u32[]{:S(2)}, u32[]{:S(2)}) %collective-permute-start.13) | collective-permute-done | bytes 32800 | tf_op jit(solution)/shard_map/ppermute | solution.py:26
  96.9 4.4 %collective-permute-done.16 = bf16[4,4,8,512]{3,2,1,0:T(8,128)(2,1)S(1)} collective-permute-done((bf16[4,4,8,512]{3,2,1,0:T(8,128)(2,1)S(1)}, bf16[4,4,8,512]{3,2,1,0:T(8,128)(2,1)S(1)}, u32[]{:S(2)}, u32[]{:S(2)}) %collective-permute-start.16) | collective-permute-done | bytes 131104 | tf_op jit(solution)/shard_map/ppermute | solution.py:36
  111.5 4.2 %collective-permute-start.23 = (bf16[4,4,8,1024]{3,2,1,0:T(8,128)(2,1)S(1)}, bf16[4,4,8,1024]{3,2,1,0:T(8,128)(2,1)S(1)}, u32[]{:S(2)}, u32[]{:S(2)}) collective-permute-start(bf16[4,4,8,1024]{3,2,1,0:T(8,128)(2,1)S(1)} %pad_maximum_fusion.6), channel_id=1, source_target_pairs={{0,8},{4,12},{8,16},{12,20},{16,24},{20,28},{1,9},{5,13},{9,17},{1... | collective-permute-start | bytes 786440 | tf_op jit(solution)/shard_map/ppermute | solution.py:36
  117.2 4.8 %collective-permute-start.20 = (bf16[4,6,1,1024]{3,2,1,0:T(2,128)(2,1)S(1)}, bf16[4,6,1,1024]{3,2,1,0:T(2,128)(2,1)S(1)}, u32[]{:S(2)}, u32[]{:S(2)}) collective-permute-start(bf16[4,6,1,1024]{3,2,1,0:T(2,128)(2,1)S(1)} %get-tuple-element.41), channel_id=1, source_target_pairs={{0,1},{1,2},{2,3},{4,5},{5,6},{6,7},{8,9},{9,10},{10,11},{12,13},{... | collective-permute-start | bytes 147464 | tf_op jit(solution)/shard_map/ppermute | solution.py:24
  123.3 5.1 %collective-permute-done.21 = bf16[4,6,1,1024]{3,2,1,0:T(2,128)(2,1)S(1)} collective-permute-done((bf16[4,6,1,1024]{3,2,1,0:T(2,128)(2,1)S(1)}, bf16[4,6,1,1024]{3,2,1,0:T(2,128)(2,1)S(1)}, u32[]{:S(2)}, u32[]{:S(2)}) %collective-permute-start.21) | collective-permute-done | bytes 49184 | tf_op jit(solution)/shard_map/ppermute | solution.py:26
  137.9 7.7 %collective-permute-start.29 = (bf16[4,4,8,1024]{3,2,1,0:T(8,128)(2,1)S(1)}, bf16[4,4,8,1024]{3,2,1,0:T(8,128)(2,1)S(1)}, u32[]{:S(2)}, u32[]{:S(2)}) collective-permute-start(bf16[4,4,8,1024]{3,2,1,0:T(8,128)(2,1)S(1)} %pad_maximum_fusion.7), channel_id=1, source_target_pairs={{0,8},{4,12},{8,16},{12,20},{16,24},{20,28},{1,9},{5,13},{9,17},{1... | collective-permute-start | bytes 786440 | tf_op jit(solution)/shard_map/ppermute | solution.py:36
  147.1 4.3 %collective-permute-start.26 = (bf16[4,6,1,1024]{3,2,1,0:T(2,128)(2,1)S(1)}, bf16[4,6,1,1024]{3,2,1,0:T(2,128)(2,1)S(1)}, u32[]{:S(2)}, u32[]{:S(2)}) collective-permute-start(bf16[4,6,1,1024]{3,2,1,0:T(2,128)(2,1)S(1)} %get-tuple-element.37), channel_id=1, source_target_pairs={{0,1},{1,2},{2,3},{4,5},{5,6},{6,7},{8,9},{9,10},{10,11},{12,13},{... | collective-permute-start | bytes 147464 | tf_op jit(solution)/shard_map/ppermute | solution.py:24
  170.3 7.7 %collective-permute-start.35 = (bf16[4,4,8,1024]{3,2,1,0:T(8,128)(2,1)S(1)}, bf16[4,4,8,1024]{3,2,1,0:T(8,128)(2,1)S(1)}, u32[]{:S(2)}, u32[]{:S(2)}) collective-permute-start(bf16[4,4,8,1024]{3,2,1,0:T(8,128)(2,1)S(1)} %pad_maximum_fusion.8), channel_id=1, source_target_pairs={{0,8},{4,12},{8,16},{12,20},{16,24},{20,28},{1,9},{5,13},{9,17},{1... | collective-permute-start | bytes 786440 | tf_op jit(solution)/shard_map/ppermute | solution.py:36
  179.4 4.3 %collective-permute-start.32 = (bf16[4,6,1,1024]{3,2,1,0:T(2,128)(2,1)S(1)}, bf16[4,6,1,1024]{3,2,1,0:T(2,128)(2,1)S(1)}, u32[]{:S(2)}, u32[]{:S(2)}) collective-permute-start(bf16[4,6,1,1024]{3,2,1,0:T(2,128)(2,1)S(1)} %get-tuple-element.33), channel_id=1, source_target_pairs={{0,1},{1,2},{2,3},{4,5},{5,6},{6,7},{8,9},{9,10},{10,11},{12,13},{... | collective-permute-start | bytes 147464 | tf_op jit(solution)/shard_map/ppermute | solution.py:24
  187.7 6.3 %collective-permute-done.34 = bf16[4,4,8,1024]{3,2,1,0:T(8,128)(2,1)S(1)} collective-permute-done((bf16[4,4,8,1024]{3,2,1,0:T(8,128)(2,1)S(1)}, bf16[4,4,8,1024]{3,2,1,0:T(8,128)(2,1)S(1)}, u32[]{:S(2)}, u32[]{:S(2)}) %collective-permute-start.34) | collective-permute-done | bytes 262176 | tf_op jit(solution)/shard_map/ppermute | solution.py:36
  205.2 4.7 %add_bitcast_fusion = f32[4096,512]{0,1:T(8,128)} fusion(f32[512,4096]{1,0:T(8,128)S(1)} %fusion.200, bf16[128,4096]{1,0:T(8,128)(2,1)S(1)} %bitcast.103, f32[128,512]{1,0:T(8,128)S(1)} %get-tuple-element.119, f32[512,128]{0,1:T(8,128)S(1)} %get-tuple-element.107, f32[128]{0:T(128)S(1)} %broadcast_multiply_fusion.2, f32[128]{0:T(128)S(1)} %copy-done.66, ...), kind=kOutput, calls=%fused_computation.4 | convolution fusion | flops 539557888 | bytes 18353152 | tf_op jit(solution)/shard_map/dot_general | solution.py:45
  209.9 9.1 %copy.25 = f32[4096,512]{1,0:T(8,128)} copy(f32[4096,512]{0,1:T(8,128)} %add_bitcast_fusion) | data formatting | bytes 16777216 | tf_op jit(solution)/shard_map/add | solution.py:259
  219.0 4.9 %multiply_reduce_fusion = f32[64,512]{1,0:T(8,128)S(1)} fusion(f32[64,512]{1,0:T(8,128)S(1)} %copy-done.13, f32[4096,512]{1,0:T(8,128)} %copy.25), kind=kLoop, calls=%fused_computation.3 | loop fusion | flops 4161536 | bytes 8650752 | tf_op jit(solution)/shard_map/reduce_sum | solution.py:260
  225.6 9.1 %reduce-scatter.5.cloned.1.call-done = f32[128,512]{1,0:T(8,128)} async-done(((f32[1024,512]{1,0:T(8,128)}), f32[128,512]{1,0:T(8,128)}) %reduce-scatter.5.cloned.1.call-update) | async-done | bytes 262160 | tf_op jit(solution)/shard_map/reduce_scatter | solution.py:285
  234.7 71.3 %reduce-scatter.3.cloned.1.call-done = f32[64,1024]{1,0:T(8,128)} async-done(((f32[512,1024]{1,0:T(8,128)}), f32[64,1024]{1,0:T(8,128)}) %reduce-scatter.3.cloned.1.call-update) | async-done | bytes 262160 | tf_op jit(solution)/shard_map/reduce_scatter | solution.py:281
  306.4 40.7 %all-reduce = (f32[512]{0:T(512)}, f32[512]{0:T(512)}, f32[512]{0:T(512)}, f32[16,512]{1,0:T(8,128)}, f32[2,512]{1,0:T(2,128)}) all-reduce(f32[512]{0:T(512)S(1)} %add_add_fusion.1, f32[512]{0:T(512)S(1)} %add_add_fusion, f32[512]{0:T(512)S(1)} %get-tuple-element.11, ...), channel_id=1, replica_groups=mesh['gx'=8,'gy'=4] {'gx','gy'}, use_global_device_ids=true, to_apply=%region_12.13 | all-reduce | flops 10752 | bytes 86016 | tf_op jit(solution)/shard_map/psum | solution.py:264
  347.0 12.5 %all-reduce.6.cloned.1.call-done = (f32[512,512]{1,0:T(8,128)}, f32[64,512]{1,0:T(8,128)}) async-done(((f32[512,512]{1,0:T(8,128)}, f32[64,512]{1,0:T(8,128)}), (f32[512,512]{1,0:T(8,128)}, f32[64,512]{1,0:T(8,128)})) %all-reduce.6.cloned.1.call-update) | async-done | bytes 1179664 | tf_op jit(solution)/shard_map/psum | solution.py:264
  359.5 34.7 %all-reduce.8.cloned.1.call-done = (f32[64,1024]{1,0:T(8,128)}, f32[128,512]{1,0:T(8,128)}) async-done(((f32[64,1024]{1,0:T(8,128)}, f32[128,512]{1,0:T(8,128)}), (f32[64,1024]{1,0:T(8,128)}, f32[128,512]{1,0:T(8,128)})) %all-reduce.8.cloned.1.call-update) | async-done | bytes 524304 | tf_op jit(solution)/shard_map/psum | solution.py:288
  (334 shorter events, 121.2 us)
Async XLA Ops:
  8.0 226.7 %reduce-scatter.5.cloned.1.call-start = ((), (), s32[]{:S(2)}) async-start(), calls=%async_computation.3 | async-start | bytes 2359296 | tf_op jit(solution)/shard_map/reduce_scatter | solution.py:285
  15.2 28.8 %collective-permute-start.5 = (bf16[4,4,8,512]{3,2,1,0:T(8,128)(2,1)}, bf16[4,4,8,512]{3,2,1,0:T(8,128)(2,1)}, u32[]{:S(2)}, u32[]{:S(2)}) collective-permute-start(bf16[4,4,8,512]{3,2,1,0:T(8,128)(2,1)} %get-tuple-element.53), channel_id=1, source_target_pairs={{0,8},{4,12},{8,16},{12,20},{16,24},{20,28},{1,9},{5,13},{9,17},{1... | collective-permute-start | bytes 393224 | tf_op jit(solution)/shard_map/ppermute | solution.py:36
  20.8 23.2 %collective-permute-start.4 = (bf16[4,4,8,512]{3,2,1,0:T(8,128)(2,1)}, bf16[4,4,8,512]{3,2,1,0:T(8,128)(2,1)}, u32[]{:S(2)}, u32[]{:S(2)}) collective-permute-start(bf16[4,4,8,512]{3,2,1,0:T(8,128)(2,1)} %get-tuple-element.53), channel_id=1, source_target_pairs={{8,0},{12,4},{16,8},{20,12},{24,16},{28,20},{9,1},{13,5},{17,9},{2... | collective-permute-start | bytes 393224 | tf_op jit(solution)/shard_map/ppermute | solution.py:36
  22.7 11.7 %collective-permute-start = (bf16[4,1,8,512]{3,2,1,0:T(8,128)(2,1)}, bf16[4,1,8,512]{3,2,1,0:T(8,128)(2,1)}, u32[]{:S(2)}, u32[]{:S(2)}) collective-permute-start(bf16[4,1,8,512]{3,2,1,0:T(8,128)(2,1)} %get-tuple-element.66), channel_id=1, source_target_pairs={{0,4},{4,8},{8,12},{12,16},{16,20},{20,24},{24,28},{1,5},{5,9},{9,... | collective-permute-start | bytes 98312 | tf_op jit(solution)/shard_map/ppermute | solution.py:24
  26.8 7.7 %collective-permute-start.1 = (bf16[4,1,8,512]{3,2,1,0:T(8,128)(2,1)}, bf16[4,1,8,512]{3,2,1,0:T(8,128)(2,1)}, u32[]{:S(2)}, u32[]{:S(2)}) collective-permute-start(bf16[4,1,8,512]{3,2,1,0:T(8,128)(2,1)} %get-tuple-element.67), channel_id=1, source_target_pairs={{4,0},{8,4},{12,8},{16,12},{20,16},{24,20},{28,24},{5,1},{9,5},{13... | collective-permute-start | bytes 98312 | tf_op jit(solution)/shard_map/ppermute | solution.py:26
  59.4 9.5 %collective-permute-start.8 = (bf16[4,6,1,512]{3,2,1,0:T(2,128)(2,1)S(1)}, bf16[4,6,1,512]{3,2,1,0:T(2,128)(2,1)S(1)}, u32[]{:S(2)}, u32[]{:S(2)}) collective-permute-start(bf16[4,6,1,512]{3,2,1,0:T(2,128)(2,1)S(1)} %get-tuple-element.74), channel_id=1, source_target_pairs={{0,1},{1,2},{2,3},{4,5},{5,6},{6,7},{8,9},{9,10},{10,11},{12,13},{... | collective-permute-start | bytes 73736 | tf_op jit(solution)/shard_map/ppermute | solution.py:24
  67.6 6.9 %collective-permute-start.10 = (bf16[4,4,8,512]{3,2,1,0:T(8,128)(2,1)S(1)}, bf16[4,4,8,512]{3,2,1,0:T(8,128)(2,1)S(1)}, u32[]{:S(2)}, u32[]{:S(2)}) collective-permute-start(bf16[4,4,8,512]{3,2,1,0:T(8,128)(2,1)S(1)} %get-tuple-element.57), channel_id=1, source_target_pairs={{8,0},{12,4},{16,8},{20,12},{24,16},{28,20},{9,1},{13,5},{17,9},{2... | collective-permute-start | bytes 393224 | tf_op jit(solution)/shard_map/ppermute | solution.py:36
  86.7 9.2 %collective-permute-start.14 = (bf16[4,6,1,512]{3,2,1,0:T(2,128)(2,1)S(1)}, bf16[4,6,1,512]{3,2,1,0:T(2,128)(2,1)S(1)}, u32[]{:S(2)}, u32[]{:S(2)}) collective-permute-start(bf16[4,6,1,512]{3,2,1,0:T(2,128)(2,1)S(1)} %get-tuple-element.70), channel_id=1, source_target_pairs={{0,1},{1,2},{2,3},{4,5},{5,6},{6,7},{8,9},{9,10},{10,11},{12,13},{... | collective-permute-start | bytes 73736 | tf_op jit(solution)/shard_map/ppermute | solution.py:24
  88.9 7.1 %collective-permute-start.15 = (bf16[4,6,1,512]{3,2,1,0:T(2,128)(2,1)S(1)}, bf16[4,6,1,512]{3,2,1,0:T(2,128)(2,1)S(1)}, u32[]{:S(2)}, u32[]{:S(2)}) collective-permute-start(bf16[4,6,1,512]{3,2,1,0:T(2,128)(2,1)S(1)} %get-tuple-element.71), channel_id=1, source_target_pairs={{1,0},{2,1},{3,2},{5,4},{6,5},{7,6},{9,8},{10,9},{11,10},{13,12},{... | collective-permute-start | bytes 73736 | tf_op jit(solution)/shard_map/ppermute | solution.py:26
  107.0 10.0 %collective-permute-start.18 = (bf16[4,1,8,1024]{3,2,1,0:T(8,128)(2,1)S(1)}, bf16[4,1,8,1024]{3,2,1,0:T(8,128)(2,1)S(1)}, u32[]{:S(2)}, u32[]{:S(2)}) collective-permute-start(bf16[4,1,8,1024]{3,2,1,0:T(8,128)(2,1)S(1)} %get-tuple-element.58), channel_id=1, source_target_pairs={{0,4},{4,8},{8,12},{12,16},{16,20},{20,24},{24,28},{1,5},{5,9},{9,... | collective-permute-start | bytes 196616 | tf_op jit(solution)/shard_map/ppermute | solution.py:24
  110.2 6.9 %collective-permute-start.19 = (bf16[4,1,8,1024]{3,2,1,0:T(8,128)(2,1)S(1)}, bf16[4,1,8,1024]{3,2,1,0:T(8,128)(2,1)S(1)}, u32[]{:S(2)}, u32[]{:S(2)}) collective-permute-start(bf16[4,1,8,1024]{3,2,1,0:T(8,128)(2,1)S(1)} %get-tuple-element.59), channel_id=1, source_target_pairs={{4,0},{8,4},{12,8},{16,12},{20,16},{24,20},{28,24},{5,1},{9,5},{13... | collective-permute-start | bytes 196616 | tf_op jit(solution)/shard_map/ppermute | solution.py:26
  111.5 17.3 %collective-permute-start.23 = (bf16[4,4,8,1024]{3,2,1,0:T(8,128)(2,1)S(1)}, bf16[4,4,8,1024]{3,2,1,0:T(8,128)(2,1)S(1)}, u32[]{:S(2)}, u32[]{:S(2)}) collective-permute-start(bf16[4,4,8,1024]{3,2,1,0:T(8,128)(2,1)S(1)} %pad_maximum_fusion.6), channel_id=1, source_target_pairs={{0,8},{4,12},{8,16},{12,20},{16,24},{20,28},{1,9},{5,13},{9,17},{1... | collective-permute-start | bytes 786440 | tf_op jit(solution)/shard_map/ppermute | solution.py:36
  115.8 13.1 %collective-permute-start.22 = (bf16[4,4,8,1024]{3,2,1,0:T(8,128)(2,1)S(1)}, bf16[4,4,8,1024]{3,2,1,0:T(8,128)(2,1)S(1)}, u32[]{:S(2)}, u32[]{:S(2)}) collective-permute-start(bf16[4,4,8,1024]{3,2,1,0:T(8,128)(2,1)S(1)} %pad_maximum_fusion.6), channel_id=1, source_target_pairs={{8,0},{12,4},{16,8},{20,12},{24,16},{28,20},{9,1},{13,5},{17,9},{2... | collective-permute-start | bytes 786440 | tf_op jit(solution)/shard_map/ppermute | solution.py:36
  134.3 12.7 %collective-permute-start.24 = (bf16[4,1,8,1024]{3,2,1,0:T(8,128)(2,1)S(1)}, bf16[4,1,8,1024]{3,2,1,0:T(8,128)(2,1)S(1)}, u32[]{:S(2)}, u32[]{:S(2)}) collective-permute-start(bf16[4,1,8,1024]{3,2,1,0:T(8,128)(2,1)S(1)} %get-tuple-element.54), channel_id=1, source_target_pairs={{0,4},{4,8},{8,12},{12,16},{16,20},{20,24},{24,28},{1,5},{5,9},{9,... | collective-permute-start | bytes 196616 | tf_op jit(solution)/shard_map/ppermute | solution.py:24
  136.6 10.4 %collective-permute-start.25 = (bf16[4,1,8,1024]{3,2,1,0:T(8,128)(2,1)S(1)}, bf16[4,1,8,1024]{3,2,1,0:T(8,128)(2,1)S(1)}, u32[]{:S(2)}, u32[]{:S(2)}) collective-permute-start(bf16[4,1,8,1024]{3,2,1,0:T(8,128)(2,1)S(1)} %get-tuple-element.55), channel_id=1, source_target_pairs={{4,0},{8,4},{12,8},{16,12},{20,16},{24,20},{28,24},{5,1},{9,5},{13... | collective-permute-start | bytes 196616 | tf_op jit(solution)/shard_map/ppermute | solution.py:26
  137.9 17.4 %collective-permute-start.29 = (bf16[4,4,8,1024]{3,2,1,0:T(8,128)(2,1)S(1)}, bf16[4,4,8,1024]{3,2,1,0:T(8,128)(2,1)S(1)}, u32[]{:S(2)}, u32[]{:S(2)}) collective-permute-start(bf16[4,4,8,1024]{3,2,1,0:T(8,128)(2,1)S(1)} %pad_maximum_fusion.7), channel_id=1, source_target_pairs={{0,8},{4,12},{8,16},{12,20},{16,24},{20,28},{1,9},{5,13},{9,17},{1... | collective-permute-start | bytes 786440 | tf_op jit(solution)/shard_map/ppermute | solution.py:36
  145.6 9.7 %collective-permute-start.28 = (bf16[4,4,8,1024]{3,2,1,0:T(8,128)(2,1)S(1)}, bf16[4,4,8,1024]{3,2,1,0:T(8,128)(2,1)S(1)}, u32[]{:S(2)}, u32[]{:S(2)}) collective-permute-start(bf16[4,4,8,1024]{3,2,1,0:T(8,128)(2,1)S(1)} %pad_maximum_fusion.7), channel_id=1, source_target_pairs={{8,0},{12,4},{16,8},{20,12},{24,16},{28,20},{9,1},{13,5},{17,9},{2... | collective-permute-start | bytes 786440 | tf_op jit(solution)/shard_map/ppermute | solution.py:36
  161.8 144.2 %reduce-scatter.3.cloned.1.call-start = ((), (), s32[]{:S(2)}) async-start(), calls=%async_computation.2 | async-start | bytes 2359296 | tf_op jit(solution)/shard_map/reduce_scatter | solution.py:281
  166.5 12.7 %collective-permute-start.30 = (bf16[4,1,8,1024]{3,2,1,0:T(8,128)(2,1)S(1)}, bf16[4,1,8,1024]{3,2,1,0:T(8,128)(2,1)S(1)}, u32[]{:S(2)}, u32[]{:S(2)}) collective-permute-start(bf16[4,1,8,1024]{3,2,1,0:T(8,128)(2,1)S(1)} %get-tuple-element.50), channel_id=1, source_target_pairs={{0,4},{4,8},{8,12},{12,16},{16,20},{20,24},{24,28},{1,5},{5,9},{9,... | collective-permute-start | bytes 196616 | tf_op jit(solution)/shard_map/ppermute | solution.py:24
  168.9 10.4 %collective-permute-start.31 = (bf16[4,1,8,1024]{3,2,1,0:T(8,128)(2,1)S(1)}, bf16[4,1,8,1024]{3,2,1,0:T(8,128)(2,1)S(1)}, u32[]{:S(2)}, u32[]{:S(2)}) collective-permute-start(bf16[4,1,8,1024]{3,2,1,0:T(8,128)(2,1)S(1)} %get-tuple-element.51), channel_id=1, source_target_pairs={{4,0},{8,4},{12,8},{16,12},{20,16},{24,20},{28,24},{5,1},{9,5},{13... | collective-permute-start | bytes 196616 | tf_op jit(solution)/shard_map/ppermute | solution.py:26
  170.3 17.4 %collective-permute-start.35 = (bf16[4,4,8,1024]{3,2,1,0:T(8,128)(2,1)S(1)}, bf16[4,4,8,1024]{3,2,1,0:T(8,128)(2,1)S(1)}, u32[]{:S(2)}, u32[]{:S(2)}) collective-permute-start(bf16[4,4,8,1024]{3,2,1,0:T(8,128)(2,1)S(1)} %pad_maximum_fusion.8), channel_id=1, source_target_pairs={{0,8},{4,12},{8,16},{12,20},{16,24},{20,28},{1,9},{5,13},{9,17},{1... | collective-permute-start | bytes 786440 | tf_op jit(solution)/shard_map/ppermute | solution.py:36
  178.0 16.0 %collective-permute-start.34 = (bf16[4,4,8,1024]{3,2,1,0:T(8,128)(2,1)S(1)}, bf16[4,4,8,1024]{3,2,1,0:T(8,128)(2,1)S(1)}, u32[]{:S(2)}, u32[]{:S(2)}) collective-permute-start(bf16[4,4,8,1024]{3,2,1,0:T(8,128)(2,1)S(1)} %pad_maximum_fusion.8), channel_id=1, source_target_pairs={{8,0},{12,4},{16,8},{20,12},{24,16},{28,20},{9,1},{13,5},{17,9},{2... | collective-permute-start | bytes 786440 | tf_op jit(solution)/shard_map/ppermute | solution.py:36
  198.4 161.1 %all-reduce.6.cloned.1.call-start = ((), (), s32[]{:S(2)}) async-start(), calls=%async_computation.4 | async-start | bytes 2359296 | tf_op jit(solution)/shard_map/psum | solution.py:264
  224.6 169.6 %all-reduce.8.cloned.1.call-start = ((), (), s32[]{:S(2)}) async-start(), calls=%async_computation.5 | async-start | bytes 1048576 | tf_op jit(solution)/shard_map/psum | solution.py:288
  (106 other events, 1587.6 us)
Sparse Core Ops, SparseCore 0:
  161.9 72.7 reduce-scatter.4
  238.2 67.7 reduce-scatter.2
Sparse Core Ops, SparseCore 1:
  224.7 134.7 all-reduce.5
  361.8 32.4 all-reduce.7
